TPU v7x, 32 devices: a whole 2x2x4 slice. The times are simulated.
32 devices in a mesh: lon: 8 (over y, x, core), lat: 4 (over z).
Axes of the slice: x: 2, y: 2, z: 4, core: 2. Of those that a mesh axis runs over, the one named last changes fastest.
Arguments:
- checkpoint: float32 [4, 256, 9600], P('lat', 'lon'), may hold values from -6 to 6
- slot_dest: int32 [4, 256], P('lat'), may hold values from -1 to 255, as said below
- kmt: int32 [640, 3840], P('lat', 'lon'), may hold values from 0 to 2, as said below
- kappa: float32 [2, 640, 3840], P(None, 'lat', 'lon'), may hold values from 0.02 to 0.2
Outputs:
- new_tracer: float32 [2, 2, 640, 3840], P(None, None, 'lat', 'lon')
- stream: float32 [640, 3840], P('lat', 'lon')
Inputs may be any that keep to these rules, and one draw needn't show every extreme that they name: `slot_dest`: in each band every value e * 32 + p is named by at most one slot; at most 4 slots of one checkpoint owner's 32 slots name one new owner e, and exactly 4 for some pair in every band. Positions that no slot names are land blocks. kmt is 0 on every point of a land block.
All inputs are finite; a program needn't handle non-finite values.
Results may differ from a plain program's by a relative error of at most 0.0001.
Values sent between devices are 32-bit elements; how exact they have to be, the bound alone decides.
No kernel may reach another device: no remote copies, remote signals or barrier semaphores. Data moves between devices by JAX's collectives and lax.ppermute only.
A program may use at most 128 MiB of HBM per device.

v0:
```python
import jax
import jax.numpy as jnp
from jax import lax
from jax.sharding import PartitionSpec as P

BH = 40
BW = 60
LEV = 2
ITERS = 3
thermal = 0.25
haline = 0.75
cabbeling = 0.05


def extended(value, sides, width, wrap):
    for axis, dim in sides:
        size, length = (lax.axis_size(axis), value.shape[dim])
        up = [(i, (i + 1) % size) for i in range(size if wrap else size - 1)]
        down = [(j, i) for i, j in up]
        last = lax.slice_in_dim(value, length - width, length, axis=dim)
        initial = lax.slice_in_dim(value, 0, width, axis=dim)
        before = lax.ppermute(last, axis, up)
        after = lax.ppermute(initial, axis, down)
        value = jnp.concatenate([before, value, after], axis=dim)
    return value


def extend(field):
    beside_all = extended(field, (("lon", 2),), 1, True)
    return extended(beside_all, (("lat", 1),), 1, False)


def operate(vector, depth, column):
    wide = extend(vector[None])[0]
    edges = wide[2:, 1:-1] + wide[:-2, 1:-1] + wide[1:-1, 2:] + wide[1:-1, :-2]
    corners = wide[2:, 2:] + wide[2:, :-2] + wide[:-2, 2:] + wide[:-2, :-2]
    return column * ((6.0 + depth) * vector - edges - 0.5 * corners)


def squares(residual):
    return lax.psum(jnp.sum(residual * residual), ("lon", "lat"))


def body(checkpoint, slot_dest, kmt, kappa):
    myself = lax.axis_index("lon")
    blocks = checkpoint[0]
    dest_all = slot_dest[0]
    slots_dev = blocks.shape[0]
    values_blk = blocks.shape[1]
    owner = jnp.where(dest_all >= 0, dest_all // slots_dev, -1)
    landing = jnp.where(dest_all >= 0, dest_all % slots_dev, 0)
    empty = jnp.zeros((slots_dev + 1, values_blk), jnp.float32)
    target = jnp.where(owner == myself, landing, slots_dev)
    placed = empty.at[target].set(lax.all_gather(blocks, "lon", axis=0, tiled=True))[:slots_dev]
    rows_dev = kmt.shape[0]
    cols_dev = kmt.shape[1]
    block_rows = rows_dev // BH
    block_cols = cols_dev // BW
    field = placed.reshape(block_rows, block_cols, 2, LEV, BH, BW)
    field = field.transpose(2, 3, 0, 4, 1, 5).reshape(2, LEV, rows_dev, cols_dev)
    levels = jnp.arange(LEV, dtype=jnp.int32)
    wet = (levels[:, None, None] < kmt[None]).astype(jnp.float32)
    tracer = field * wet
    stacked = jnp.concatenate([tracer.reshape(2 * LEV, rows_dev, cols_dev), wet, kappa], axis=0)
    wide = extend(stacked)
    tracer_w = wide[: 2 * LEV].reshape(2, LEV, rows_dev + 2, cols_dev + 2)
    wet_w = wide[2 * LEV : 3 * LEV]
    kappa_w = wide[3 * LEV :]
    tracer_c = tracer_w[..., 1:-1, 1:-1]
    wet_c = wet_w[:, 1:-1, 1:-1]
    kappa_c = kappa_w[:, 1:-1, 1:-1]
    change = jnp.zeros_like(tracer)
    for step_y, step_x in ((0, 1), (0, -1), (1, 0), (-1, 0)):
        rows = slice(1 + step_y, 1 + step_y + rows_dev)
        cols = slice(1 + step_x, 1 + step_x + cols_dev)
        face = 0.5 * (kappa_c + kappa_w[:, rows, cols]) * wet_c * wet_w[:, rows, cols]
        change = change + face * (tracer_w[..., rows, cols] - tracer_c)
    new_tracer = wet * (tracer + change)
    thickness = 1.0 + 0.5 * jnp.arange(LEV, dtype=jnp.float32)
    temp = new_tracer[0]
    salt = new_tracer[1]
    density = wet * (haline * salt - thermal * temp - cabbeling * temp * temp)
    forcing = jnp.sum(thickness[:, None, None] * density, axis=0)
    depth = jnp.sum(thickness[:, None, None] * wet, axis=0)
    column = (kmt > 0).astype(jnp.float32)
    stream = jnp.zeros_like(forcing)
    residual = column * forcing
    direction = residual
    norm_now = squares(residual)
    for step in range(ITERS):
        image = operate(direction, depth, column)
        alpha = norm_now / lax.psum(jnp.sum(direction * image), ("lon", "lat"))
        stream = stream + alpha * direction
        residual = residual - alpha * image
        norm_next = squares(residual)
        direction = residual + norm_next / norm_now * direction
        norm_now = norm_next
    return (new_tracer, stream)


def solution(mesh):
    placed = (P("lat", "lon", None), P("lat", None), P("lat", "lon"), P(None, "lat", "lon"))
    return jax.shard_map(
        body,
        mesh=mesh,
        in_specs=placed,
        out_specs=(P(None, None, "lat", "lon"), P("lat", "lon")),
        check_vma=False,
    )
```

profile of v0, /device:TPU:0, one launch (start us, length us, event | category | flops | bytes accessed | tf_op | source)
XLA Modules:
  0.0 378.9 jit_solution(3048188095001395048)
XLA Ops:
  7.2 0.7 all-gather.3.cloned.1.call-update
  7.9 0.7 compare_select_fusion
  8.7 64.3 %all-gather.3.cloned.1.call-done = f32[1,256,9600]{2,1,0:T(8,128)} async-done(((f32[1,32,9600]{2,1,0:T(8,128)}), f32[1,256,9600]{2,1,0:T(8,128)}) %all-gather.3.cloned.1.call-update) | async-done | bytes 9830416 | tf_op jit(solution)/shard_map/all_gather | solution.py:54
  73.0 10.2 %scatter_custom_fusion = f32[33,9600]{1,0:T(8,128)S(1)} fusion(s32[256]{0:T(256)S(1)} %bitcast.51, f32[1,256,9600]{2,1,0:T(8,128)} %all-gather.3.cloned.1.call-done, f32[]{:T(128)} %constant.51.clone.1), kind=kCustom, calls=%fused_computation.1 | custom fusion | bytes 11097604 | tf_op jit(solution)/shard_map/scatter | solution.py:54
  83.3 5.4 %reshape.159 = f32[4,8,2,2,40,60]{5,4,3,2,1,0:T(8,128)} reshape(f32[32,9600]{1,0:T(8,128)S(1)} %slice.258) | data formatting | bytes 2457600 | tf_op jit(solution)/shard_map/reshape | solution.py:59
  88.7 3.3 copy.8
  92.0 1.5 copy-done
  93.5 1.7 reshape.161
  95.3 1.6 bitcast_multiply_fusion
  97.8 1.3 collective-permute-start
  99.1 2.9 reshape.160
  102.1 1.0 collective-permute-done.1
  103.7 1.0 pad_maximum_fusion.29
  104.7 1.3 collective-permute-start.3
  106.0 0.8 fusion.27
  106.9 4.5 %collective-permute-start.2 = (f32[8,1,482]{2,1,0:T(1,128)S(1)}, f32[8,1,482]{2,1,0:T(1,128)S(1)}, u32[]{:S(2)}, u32[]{:S(2)}) collective-permute-start(f32[8,1,482]{2,1,0:T(1,128)S(1)} %get-tuple-element.15), channel_id=1, source_target_pairs={{0,1},{1,2},{2,3},{4,5},{5,6},{6,7},{8,9},{9,10},{10,11},{12,13},{... | collective-permute-start | bytes 46280 | tf_op jit(solution)/shard_map/ppermute | solution.py:22
  111.4 0.4 fusion.21
  111.8 1.0 collective-permute-done.2
  113.2 0.5 pad_maximum_fusion
  113.8 0.8 copy-done.6
  114.5 1.4 fusion.5
  116.4 0.7 copy-done.5
  117.2 2.6 collective-permute-start.5
  119.8 2.5 collective-permute-done.4
  122.5 4.2 %collective-permute-start.6 = (f32[1,1,482]{2,1,0:T(1,128)S(1)}, f32[1,1,482]{2,1,0:T(1,128)S(1)}, u32[]{:S(2)}, u32[]{:S(2)}) collective-permute-start(f32[1,1,482]{2,1,0:T(1,128)S(1)} %get-tuple-element.25), channel_id=1, source_target_pairs={{0,1},{1,2},{2,3},{4,5},{5,6},{6,7},{8,9},{9,10},{10,11},{12,13},{... | collective-permute-start | bytes 5792 | tf_op jit(solution)/shard_map/ppermute | solution.py:22
  126.7 1.5 collective-permute-start.7
  128.2 3.9 %collective-permute-done.7 = f32[1,1,482]{2,1,0:T(1,128)S(1)} collective-permute-done((f32[1,1,482]{2,1,0:T(1,128)S(1)}, f32[1,1,482]{2,1,0:T(1,128)S(1)}, u32[]{:S(2)}, u32[]{:S(2)}) %collective-permute-start.7) | collective-permute-done | bytes 1960 | tf_op jit(solution)/shard_map/ppermute | solution.py:23
  132.3 1.1 multiply_reduce_fusion.3
  133.4 39.5 %all-reduce = (f32[]{:T(128)}, f32[]{:T(128)}) all-reduce(f32[]{:T(128)} %get-tuple-element.3, f32[]{:T(128)} %get-tuple-element.2), channel_id=1, replica_groups=mesh['lon'=8,'lat'=4] {'lon','lat'}, use_global_device_ids=true, to_apply=%region_3.4 | all-reduce | flops 2 | bytes 16 | tf_op jit(solution)/shard_map/psum | solution.py:41
  174.3 0.7 multiply_reduce_fusion.2
  175.0 39.9 %psum.44 = f32[]{:T(128)} all-reduce(f32[]{:T(128)} %get-tuple-element.10), channel_id=1, replica_groups=mesh['lon'=8,'lat'=4] {'lon','lat'}, use_global_device_ids=true, to_apply=%region_8.9 | all-reduce | flops 1 | bytes 8 | tf_op jit(solution)/shard_map/psum | solution.py:41
  216.4 2.6 collective-permute-start.9
  219.0 2.1 collective-permute-done.8
  221.2 3.5 collective-permute-start.10
  224.7 1.3 collective-permute-start.11
  226.0 4.2 %collective-permute-done.11 = f32[1,1,482]{2,1,0:T(1,128)S(1)} collective-permute-done((f32[1,1,482]{2,1,0:T(1,128)S(1)}, f32[1,1,482]{2,1,0:T(1,128)S(1)}, u32[]{:S(2)}, u32[]{:S(2)}) %collective-permute-start.11) | collective-permute-done | bytes 1960 | tf_op jit(solution)/shard_map/ppermute | solution.py:23
  230.4 1.1 multiply_reduce_fusion.1
  231.5 40.0 %psum.45 = f32[]{:T(128)} all-reduce(f32[]{:T(128)} %get-tuple-element.8), channel_id=1, replica_groups=mesh['lon'=8,'lat'=4] {'lon','lat'}, use_global_device_ids=true, to_apply=%region_10.11 | all-reduce | flops 1 | bytes 8 | tf_op jit(solution)/shard_map/psum | solution.py:92
  272.8 0.7 multiply_reduce_fusion
  273.5 40.8 %psum.46 = f32[]{:T(128)} all-reduce(f32[]{:T(128)} %multiply_reduce_fusion), channel_id=1, replica_groups=mesh['lon'=8,'lat'=4] {'lon','lat'}, use_global_device_ids=true, to_apply=%region_12.13 | all-reduce | flops 1 | bytes 8 | tf_op jit(solution)/shard_map/psum | solution.py:41
  315.8 2.6 collective-permute-start.13
  318.4 2.1 collective-permute-done.12
  320.6 3.3 collective-permute-start.14
  323.9 1.3 collective-permute-start.15
  325.2 4.2 %collective-permute-done.15 = f32[1,1,482]{2,1,0:T(1,128)S(1)} collective-permute-done((f32[1,1,482]{2,1,0:T(1,128)S(1)}, f32[1,1,482]{2,1,0:T(1,128)S(1)}, u32[]{:S(2)}, u32[]{:S(2)}) %collective-permute-start.15) | collective-permute-done | bytes 1960 | tf_op jit(solution)/shard_map/ppermute | solution.py:23
  329.6 1.1 fusion.35
  330.7 39.3 %psum.47 = f32[]{:T(128)} all-reduce(f32[]{:T(128)} %fusion.35), channel_id=1, replica_groups=mesh['lon'=8,'lat'=4] {'lon','lat'}, use_global_device_ids=true, to_apply=%region_14.15 | all-reduce | flops 1 | bytes 8 | tf_op jit(solution)/shard_map/psum | solution.py:92
  371.2 0.8 multiply_add_fusion
  (46 shorter events, 3.8 us)
Async XLA Ops:
  7.2 1.4 copy-start.3
  7.2 65.8 %all-gather.3.cloned.1.call-start = ((), (), s32[]{:S(2)}) async-start(), calls=%async_computation | async-start | bytes 11059200 | tf_op jit(solution)/shard_map/all_gather | solution.py:54
  92.0 1.5 copy-start
  95.3 1.6 copy-start.1
  97.8 5.6 %collective-permute-start = (f32[8,160,1]{1,0,2:T(8,128)S(1)}, f32[8,160,1]{1,0,2:T(8,128)S(1)}, u32[]{:S(2)}, u32[]{:S(2)}) collective-permute-start(f32[8,160,1]{1,0,2:T(8,128)S(1)} %copy.10), channel_id=1, source_target_pairs={{4,0},{8,4},{12,8},{16,12},{20,16},{24,20},{28,24},{0,28},{5,1},{9... | collective-permute-start | bytes 15368 | tf_op jit(solution)/shard_map/ppermute | solution.py:23
  99.1 4.0 %collective-permute-start.1 = (f32[8,160,1]{1,0,2:T(8,128)S(1)}, f32[8,160,1]{1,0,2:T(8,128)S(1)}, u32[]{:S(2)}, u32[]{:S(2)}) collective-permute-start(f32[8,160,1]{1,0,2:T(8,128)S(1)} %copy.12), channel_id=1, source_target_pairs={{0,4},{4,8},{8,12},{12,16},{16,20},{20,24},{24,28},{28,0},{1,5},{5... | collective-permute-start | bytes 15368 | tf_op jit(solution)/shard_map/ppermute | solution.py:22
  103.7 2.3 copy-start.2
  103.7 2.3 copy-start.4
  104.7 6.7 %collective-permute-start.3 = (f32[8,1,482]{2,1,0:T(1,128)S(1)}, f32[8,1,482]{2,1,0:T(1,128)S(1)}, u32[]{:S(2)}, u32[]{:S(2)}) collective-permute-start(f32[8,1,482]{2,1,0:T(1,128)S(1)} %get-tuple-element.16), channel_id=1, source_target_pairs={{1,0},{2,1},{3,2},{5,4},{6,5},{7,6},{9,8},{10,9},{11,10},{13,12},{... | collective-permute-start | bytes 46280 | tf_op jit(solution)/shard_map/ppermute | solution.py:23
  106.9 6.0 %collective-permute-start.2 = (f32[8,1,482]{2,1,0:T(1,128)S(1)}, f32[8,1,482]{2,1,0:T(1,128)S(1)}, u32[]{:S(2)}, u32[]{:S(2)}) collective-permute-start(f32[8,1,482]{2,1,0:T(1,128)S(1)} %get-tuple-element.15), channel_id=1, source_target_pairs={{0,1},{1,2},{2,3},{4,5},{5,6},{6,7},{8,9},{9,10},{10,11},{12,13},{... | collective-permute-start | bytes 46280 | tf_op jit(solution)/shard_map/ppermute | solution.py:22
  113.2 1.3 copy-start.6
  116.0 1.1 copy-start.5
  117.1 5.2 %collective-permute-start.4 = (f32[1,160,1]{2,1,0:T(8,128)S(1)}, f32[1,160,1]{2,1,0:T(8,128)S(1)}, u32[]{:S(2)}, u32[]{:S(2)}) collective-permute-start(f32[1,160,1]{2,1,0:T(8,128)S(1)} %get-tuple-element.31), channel_id=1, source_target_pairs={{0,4},{4,8},{8,12},{12,16},{16,20},{20,24},{24,28},{28,0},{1,5},{5... | collective-permute-start | bytes 1928 | tf_op jit(solution)/shard_map/ppermute | solution.py:22
  117.2 5.2 %collective-permute-start.5 = (f32[1,160,1]{2,1,0:T(8,128)S(1)}, f32[1,160,1]{2,1,0:T(8,128)S(1)}, u32[]{:S(2)}, u32[]{:S(2)}) collective-permute-start(f32[1,160,1]{2,1,0:T(8,128)S(1)} %get-tuple-element.32), channel_id=1, source_target_pairs={{4,0},{8,4},{12,8},{16,12},{20,16},{24,20},{28,24},{0,28},{5,1},{9... | collective-permute-start | bytes 1928 | tf_op jit(solution)/shard_map/ppermute | solution.py:23
  122.5 5.7 %collective-permute-start.6 = (f32[1,1,482]{2,1,0:T(1,128)S(1)}, f32[1,1,482]{2,1,0:T(1,128)S(1)}, u32[]{:S(2)}, u32[]{:S(2)}) collective-permute-start(f32[1,1,482]{2,1,0:T(1,128)S(1)} %get-tuple-element.25), channel_id=1, source_target_pairs={{0,1},{1,2},{2,3},{4,5},{5,6},{6,7},{8,9},{9,10},{10,11},{12,13},{... | collective-permute-start | bytes 5792 | tf_op jit(solution)/shard_map/ppermute | solution.py:22
  126.7 5.5 %collective-permute-start.7 = (f32[1,1,482]{2,1,0:T(1,128)S(1)}, f32[1,1,482]{2,1,0:T(1,128)S(1)}, u32[]{:S(2)}, u32[]{:S(2)}) collective-permute-start(f32[1,1,482]{2,1,0:T(1,128)S(1)} %get-tuple-element.26), channel_id=1, source_target_pairs={{1,0},{2,1},{3,2},{5,4},{6,5},{7,6},{9,8},{10,9},{11,10},{13,12},{... | collective-permute-start | bytes 5792 | tf_op jit(solution)/shard_map/ppermute | solution.py:23
  216.3 4.8 %collective-permute-start.8 = (f32[1,160,1]{2,1,0:T(8,128)S(1)}, f32[1,160,1]{2,1,0:T(8,128)S(1)}, u32[]{:S(2)}, u32[]{:S(2)}) collective-permute-start(f32[1,160,1]{2,1,0:T(8,128)S(1)} %get-tuple-element.29), channel_id=1, source_target_pairs={{0,4},{4,8},{8,12},{12,16},{16,20},{20,24},{24,28},{28,0},{1,5},{5... | collective-permute-start | bytes 1928 | tf_op jit(solution)/shard_map/ppermute | solution.py:22
  216.4 4.8 %collective-permute-start.9 = (f32[1,160,1]{2,1,0:T(8,128)S(1)}, f32[1,160,1]{2,1,0:T(8,128)S(1)}, u32[]{:S(2)}, u32[]{:S(2)}) collective-permute-start(f32[1,160,1]{2,1,0:T(8,128)S(1)} %get-tuple-element.30), channel_id=1, source_target_pairs={{4,0},{8,4},{12,8},{16,12},{20,16},{24,20},{28,24},{0,28},{5,1},{9... | collective-permute-start | bytes 1928 | tf_op jit(solution)/shard_map/ppermute | solution.py:23
  221.2 4.8 %collective-permute-start.10 = (f32[1,1,482]{2,1,0:T(1,128)S(1)}, f32[1,1,482]{2,1,0:T(1,128)S(1)}, u32[]{:S(2)}, u32[]{:S(2)}) collective-permute-start(f32[1,1,482]{2,1,0:T(1,128)S(1)} %get-tuple-element.23), channel_id=1, source_target_pairs={{0,1},{1,2},{2,3},{4,5},{5,6},{6,7},{8,9},{9,10},{10,11},{12,13},{... | collective-permute-start | bytes 5792 | tf_op jit(solution)/shard_map/ppermute | solution.py:22
  224.7 5.5 %collective-permute-start.11 = (f32[1,1,482]{2,1,0:T(1,128)S(1)}, f32[1,1,482]{2,1,0:T(1,128)S(1)}, u32[]{:S(2)}, u32[]{:S(2)}) collective-permute-start(f32[1,1,482]{2,1,0:T(1,128)S(1)} %get-tuple-element.24), channel_id=1, source_target_pairs={{1,0},{2,1},{3,2},{5,4},{6,5},{7,6},{9,8},{10,9},{11,10},{13,12},{... | collective-permute-start | bytes 5792 | tf_op jit(solution)/shard_map/ppermute | solution.py:23
  315.7 4.8 %collective-permute-start.12 = (f32[1,160,1]{2,1,0:T(8,128)S(1)}, f32[1,160,1]{2,1,0:T(8,128)S(1)}, u32[]{:S(2)}, u32[]{:S(2)}) collective-permute-start(f32[1,160,1]{2,1,0:T(8,128)S(1)} %get-tuple-element.27), channel_id=1, source_target_pairs={{0,4},{4,8},{8,12},{12,16},{16,20},{20,24},{24,28},{28,0},{1,5},{5... | collective-permute-start | bytes 1928 | tf_op jit(solution)/shard_map/ppermute | solution.py:22
  315.8 4.8 %collective-permute-start.13 = (f32[1,160,1]{2,1,0:T(8,128)S(1)}, f32[1,160,1]{2,1,0:T(8,128)S(1)}, u32[]{:S(2)}, u32[]{:S(2)}) collective-permute-start(f32[1,160,1]{2,1,0:T(8,128)S(1)} %get-tuple-element.28), channel_id=1, source_target_pairs={{4,0},{8,4},{12,8},{16,12},{20,16},{24,20},{28,24},{0,28},{5,1},{9... | collective-permute-start | bytes 1928 | tf_op jit(solution)/shard_map/ppermute | solution.py:23
  320.6 4.6 %collective-permute-start.14 = (f32[1,1,482]{2,1,0:T(1,128)S(1)}, f32[1,1,482]{2,1,0:T(1,128)S(1)}, u32[]{:S(2)}, u32[]{:S(2)}) collective-permute-start(f32[1,1,482]{2,1,0:T(1,128)S(1)} %get-tuple-element.21), channel_id=1, source_target_pairs={{0,1},{1,2},{2,3},{4,5},{5,6},{6,7},{8,9},{9,10},{10,11},{12,13},{... | collective-permute-start | bytes 5792 | tf_op jit(solution)/shard_map/ppermute | solution.py:22
  323.9 5.5 %collective-permute-start.15 = (f32[1,1,482]{2,1,0:T(1,128)S(1)}, f32[1,1,482]{2,1,0:T(1,128)S(1)}, u32[]{:S(2)}, u32[]{:S(2)}) collective-permute-start(f32[1,1,482]{2,1,0:T(1,128)S(1)} %get-tuple-element.22), channel_id=1, source_target_pairs={{1,0},{2,1},{3,2},{5,4},{6,5},{7,6},{9,8},{10,9},{11,10},{13,12},{... | collective-permute-start | bytes 5792 | tf_op jit(solution)/shard_map/ppermute | solution.py:23
Sparse Core Ops, SparseCore 0:
  9.9 63.0 all-gather.2
where the time goes:
time: 380 us; the launch traced here: 379 us
  blocking collectives  199 us (52%)
  waiting for transfers between devices  86.1 us (23%)
  starting transfers between devices  30.4 us (8%)
  local copies, waits for them, and re-layouts  28.1 us (7%)
  between operations  20.9 us (6%)
  other arithmetic  14 us (4%)
    psum x3, blocking collectives, squares(): return lax.psum(jnp.sum(residual * residual), ('lon', 'lat'))  120 us
    psum x2, blocking collectives, body(): alpha = norm_now / lax.psum(jnp.sum(direction * image), ('lon', 'lat'))  79.2 us
    all_gather x1, waiting for transfers between devices, body(): lax.all_gather(blocks, 'lon', axis=0, tiled=True)  64.3 us
    ppermute x8, starting transfers between devices, extended(): before = lax.ppermute(last, axis, up)  15.7 us
    ppermute x8, starting transfers between devices, extended(): after = lax.ppermute(initial, axis, down)  14.6 us
    ppermute x8, waiting for transfers between devices, extended(): after = lax.ppermute(initial, axis, down)  12.3 us
    scatter x1, local copies, waits for them, and re-layouts, body(): empty.at[target].set(lax.all_gather(blocks, 'lon', axis=0, tiled=True))  10.2 us
    ppermute x8, waiting for transfers between devices, extended(): before = lax.ppermute(last, axis, up)  8.86 us
  transfers between devices with their start and end apart: 17, of which 9 were waited for; matrix products, arithmetic and copies ran while one was open for 1% of the time, Pallas kernels for 0%

commit v1 on v0

--- a/solution.py
+++ b/solution.py
@@ -10,6 +10,28 @@
 thermal = 0.25
 haline = 0.75
 cabbeling = 0.05
+
+
+def joined_along(blocks, dim):
+    dims = list(blocks.shape[1:])
+    dims[dim] *= blocks.shape[0]
+    return jnp.moveaxis(blocks, 0, dim).reshape(dims)
+
+
+def ring_gather(x, axis, dim):
+    length = lax.axis_size(axis)
+    pairs = [(i, (i + 1) % length) for i in range(length)]
+    back = [(b, a) for a, b in pairs]
+    lower, upper = ([], [])
+    for hop in range(length - 1):
+        if hop % 2 == 0:
+            lower.append(lax.ppermute(lower[-1] if lower else x, axis, pairs))
+        else:
+            upper.append(lax.ppermute(upper[-1] if upper else x, axis, back))
+    blocks = jnp.stack([*lower[::-1], x, *upper])
+    shift = lax.axis_index(axis) - len(lower)
+    blocks = blocks[(jnp.arange(length) - shift) % length]
+    return joined_along(blocks, dim)
 
 
 def extended(value, sides, width, wrap):
@@ -51,7 +73,7 @@
     landing = jnp.where(dest_all >= 0, dest_all % slots_dev, 0)
     empty = jnp.zeros((slots_dev + 1, values_blk), jnp.float32)
     target = jnp.where(owner == myself, landing, slots_dev)
-    placed = empty.at[target].set(lax.all_gather(blocks, "lon", axis=0, tiled=True))[:slots_dev]
+    placed = empty.at[target].set(ring_gather(blocks, "lon", 0))[:slots_dev]
     rows_dev = kmt.shape[0]
     cols_dev = kmt.shape[1]
     block_rows = rows_dev // BH

time: 380 us -> 430 us (1.13)
  waiting for transfers between devices: 86.1 us -> 115 us
  local copies, waits for them, and re-layouts: 28.1 us -> 51 us
  between operations: 20.9 us -> 7.51 us
  starting transfers between devices: 30.4 us -> 39.6 us
    ppermute x0 -> x7, waiting for transfers between devices: none -> 94.8 us  [the longest x4 94.8 us: ring_gather(): lower.append(lax.ppermute(lower[-1] if lower else x, axis, pairs))]
    all_gather x1 -> x0, waiting for transfers between devices: 64.3 us -> none  [body(): lax.all_gather(blocks, 'lon', axis=0, tiled=True)]
    unnamed x14 -> x25, local copies, waits for them, and re-layouts: 2.96 us -> 16.5 us
    gather x0 -> x1, local copies, waits for them, and re-layouts: none -> 8.74 us  [ring_gather(): blocks = blocks[(jnp.arange(length) - shift) % length]]
    ppermute x0 -> x7, starting transfers between devices: none -> 7.54 us  [the longest x3 6.99 us: ring_gather(): upper.append(lax.ppermute(upper[-1] if upper else x, axis, back))]
  transfers between devices with their start and end apart: 17 -> 23, of which waited for: 9 -> 12; matrix products, arithmetic and copies ran while one was open for 1% -> 4% of each run, Pallas kernels for 0% -> 0%
where the time goes in v1:
time: 430 us; the launch traced here: 429 us
  blocking collectives  200 us (47%)
  waiting for transfers between devices  115 us (27%)
  local copies, waits for them, and re-layouts  51 us (12%)
  starting transfers between devices  39.6 us (9%)
  other arithmetic  15.3 us (4%)
  between operations  7.51 us (2%)
    psum x3, blocking collectives, squares(): return lax.psum(jnp.sum(residual * residual), ('lon', 'lat'))  120 us
    ppermute x4, waiting for transfers between devices, ring_gather(): lower.append(lax.ppermute(lower[-1] if lower else x, axis, pairs))  94.8 us
    psum x2, blocking collectives, body(): alpha = norm_now / lax.psum(jnp.sum(direction * image), ('lon', 'lat'))  79.6 us
    ppermute x8, starting transfers between devices, extended(): before = lax.ppermute(last, axis, up)  18.8 us
    unnamed x25, local copies, waits for them, and re-layouts  16.5 us
    ppermute x8, starting transfers between devices, extended(): after = lax.ppermute(initial, axis, down)  13.3 us
    ppermute x8, waiting for transfers between devices, extended(): after = lax.ppermute(initial, axis, down)  12.3 us
    scatter x1, local copies, waits for them, and re-layouts, body(): placed = empty.at[target].set(ring_gather(blocks, 'lon', 0))[:slots_dev]  9.6 us
  transfers between devices with their start and end apart: 23, of which 12 were waited for; matrix products, arithmetic and copies ran while one was open for 4% of the time, Pallas kernels for 0%

profile of v1, /device:TPU:0, one launch (start us, length us, event | category | flops | bytes accessed | tf_op | source)
XLA Modules:
  0.0 428.7 jit_solution(5009465108225308207)
XLA Ops:
  1.2 17.5 %collective-permute-done = f32[32,9600]{1,0:T(8,128)S(1)} collective-permute-done((f32[32,9600]{1,0:T(8,128)}, f32[32,9600]{1,0:T(8,128)S(1)}, u32[]{:S(2)}, u32[]{:S(2)}) %collective-permute-start) | collective-permute-done | bytes 1228832 | tf_op jit(solution)/shard_map/ppermute | solution.py:28
  18.7 2.6 collective-permute-start.4
  21.3 25.7 %collective-permute-done.1 = f32[32,9600]{1,0:T(8,128)S(1)} collective-permute-done((f32[32,9600]{1,0:T(8,128)S(1)}, f32[32,9600]{1,0:T(8,128)S(1)}, u32[]{:S(2)}, u32[]{:S(2)}) %collective-permute-start.1) | collective-permute-done | bytes 1228832 | tf_op jit(solution)/shard_map/ppermute | solution.py:28
  48.0 1.6 collective-permute-start.5
  49.7 26.3 %collective-permute-done.2 = f32[32,9600]{1,0:T(8,128)} collective-permute-done((f32[32,9600]{1,0:T(8,128)S(1)}, f32[32,9600]{1,0:T(8,128)}, u32[]{:S(2)}, u32[]{:S(2)}) %collective-permute-start.2) | collective-permute-done | bytes 1228832 | tf_op jit(solution)/shard_map/ppermute | solution.py:28
  77.8 2.7 collective-permute-start.6
  80.5 25.3 %collective-permute-done.3 = f32[32,9600]{1,0:T(8,128)} collective-permute-done((f32[32,9600]{1,0:T(8,128)}, f32[32,9600]{1,0:T(8,128)}, u32[]{:S(2)}, u32[]{:S(2)}) %collective-permute-start.3) | collective-permute-done | bytes 1228832 | tf_op jit(solution)/shard_map/ppermute | solution.py:28
  105.8 2.4 bitcast_dynamic-update-slice_fusion.6
  108.2 2.5 bitcast_dynamic-update-slice_fusion.5
  110.8 1.1 bitcast_dynamic-update-slice_fusion.4
  111.9 1.1 bitcast_dynamic-update-slice_fusion.3
  113.6 1.1 constant_dynamic-update-slice_fusion
  114.8 1.1 bitcast_dynamic-update-slice_fusion.2
  115.9 2.5 bitcast_dynamic-update-slice_fusion.1
  118.4 1.2 bitcast_dynamic-update-slice_fusion
  119.6 8.7 %gather_fusion = f32[8,32,9600]{2,1,0:T(8,128)} fusion(f32[8,32,9600]{2,1,0:T(8,128)} %bitcast_dynamic-update-slice_fusion, s32[1024]{0:T(1024)S(1)} %pad_clamp_fusion), kind=kCustom, calls=%fused_computation | custom fusion | bytes 19660832 | tf_op jit(solution)/shard_map/gather | solution.py:33
  128.3 9.6 %scatter_custom_fusion = f32[33,9600]{1,0:T(8,128)S(1)} fusion(s32[256]{0:T(256)S(1)} %bitcast.68, f32[256,9600]{1,0:T(8,128)} %bitcast.65, f32[]{:T(128)} %constant.67.clone.1), kind=kCustom, calls=%fused_computation.30 | custom fusion | bytes 1267712 | tf_op jit(solution)/shard_map/scatter | solution.py:76
  138.0 5.4 %reshape.212 = f32[4,8,2,2,40,60]{5,4,3,2,1,0:T(8,128)} reshape(f32[32,9600]{1,0:T(8,128)S(1)} %slice.260) | data formatting | bytes 2457600 | tf_op jit(solution)/shard_map/reshape | solution.py:81
  143.4 3.3 copy.8
  146.7 1.5 copy-done
  148.2 1.7 reshape.214
  150.0 1.6 bitcast_multiply_fusion
  153.0 2.9 reshape.213
  157.8 1.3 collective-permute-start.10
  160.0 7.0 %collective-permute-start.9 = (f32[8,1,482]{2,1,0:T(1,128)S(1)}, f32[8,1,482]{2,1,0:T(1,128)S(1)}, u32[]{:S(2)}, u32[]{:S(2)}) collective-permute-start(f32[8,1,482]{2,1,0:T(1,128)S(1)} %get-tuple-element.15), channel_id=1, source_target_pairs={{0,1},{1,2},{2,3},{4,5},{5,6},{6,7},{8,9},{9,10},{10,11},{12,13},{... | collective-permute-start | bytes 46280 | tf_op jit(solution)/shard_map/ppermute | solution.py:44
  170.1 1.4 fusion.3
  172.8 2.6 collective-permute-start.12
  175.4 2.8 collective-permute-done.11
  178.3 4.2 collective-permute-start.13
  182.5 1.5 collective-permute-start.14
  184.0 3.9 collective-permute-done.14
  188.1 1.2 multiply_reduce_fusion.3
  189.4 40.1 %all-reduce = (f32[]{:T(128)}, f32[]{:T(128)}) all-reduce(f32[]{:T(128)} %get-tuple-element.3, f32[]{:T(128)} %get-tuple-element.2), channel_id=1, replica_groups=mesh['lon'=8,'lat'=4] {'lon','lat'}, use_global_device_ids=true, to_apply=%region_3.4 | all-reduce | flops 2 | bytes 16 | tf_op jit(solution)/shard_map/psum | solution.py:63
  231.4 39.4 %psum.44 = f32[]{:T(128)} all-reduce(f32[]{:T(128)} %get-tuple-element.10), channel_id=1, replica_groups=mesh['lon'=8,'lat'=4] {'lon','lat'}, use_global_device_ids=true, to_apply=%region_8.9 | all-reduce | flops 1 | bytes 8 | tf_op jit(solution)/shard_map/psum | solution.py:63
  272.3 2.6 collective-permute-start.16
  275.0 2.1 collective-permute-done.15
  277.2 3.6 collective-permute-start.17
  280.8 1.3 collective-permute-start.18
  282.1 4.2 collective-permute-done.18
  286.4 1.2 multiply_reduce_fusion.1
  287.6 40.1 %psum.45 = f32[]{:T(128)} all-reduce(f32[]{:T(128)} %get-tuple-element.8), channel_id=1, replica_groups=mesh['lon'=8,'lat'=4] {'lon','lat'}, use_global_device_ids=true, to_apply=%region_10.11 | all-reduce | flops 1 | bytes 8 | tf_op jit(solution)/shard_map/psum | solution.py:114
  329.8 40.8 %psum.46 = f32[]{:T(128)} all-reduce(f32[]{:T(128)} %multiply_reduce_fusion), channel_id=1, replica_groups=mesh['lon'=8,'lat'=4] {'lon','lat'}, use_global_device_ids=true, to_apply=%region_12.13 | all-reduce | flops 1 | bytes 8 | tf_op jit(solution)/shard_map/psum | solution.py:63
  372.2 2.6 collective-permute-start.20
  374.8 2.1 collective-permute-done.19
  377.0 3.3 collective-permute-start.21
  380.3 1.3 collective-permute-start.22
  381.6 4.2 collective-permute-done.22
  387.1 39.4 %psum.47 = f32[]{:T(128)} all-reduce(f32[]{:T(128)} %fusion.34), channel_id=1, replica_groups=mesh['lon'=8,'lat'=4] {'lon','lat'}, use_global_device_ids=true, to_apply=%region_14.15 | all-reduce | flops 1 | bytes 8 | tf_op jit(solution)/shard_map/psum | solution.py:114
  (72 shorter events, 17.1 us)
Async XLA Ops:
  0.6 18.0 %collective-permute-start = (f32[32,9600]{1,0:T(8,128)}, f32[32,9600]{1,0:T(8,128)S(1)}, u32[]{:S(2)}, u32[]{:S(2)}) collective-permute-start(f32[32,9600]{1,0:T(8,128)} %bitcast.66), channel_id=1, source_target_pairs={{0,4},{4,8},{8,12},{12,16},{16,20},{20,24},{24,28},{28,0},{1,5},{5... | collective-permute-start | bytes 3686408 | tf_op jit(solution)/shard_map/ppermute | solution.py:28
  18.7 28.3 %collective-permute-start.1 = (f32[32,9600]{1,0:T(8,128)S(1)}, f32[32,9600]{1,0:T(8,128)S(1)}, u32[]{:S(2)}, u32[]{:S(2)}) collective-permute-start(f32[32,9600]{1,0:T(8,128)S(1)} %collective-permute-done), channel_id=1, source_target_pairs={{0,4},{4,8},{8,12},{12,16},{16,20},{20,24},{24,28},{28,0},{1,5},{5... | collective-permute-start | bytes 3686408 | tf_op jit(solution)/shard_map/ppermute | solution.py:28
  18.7 28.3 %collective-permute-start.4 = (f32[32,9600]{1,0:T(8,128)}, f32[32,9600]{1,0:T(8,128)S(1)}, u32[]{:S(2)}, u32[]{:S(2)}) collective-permute-start(f32[32,9600]{1,0:T(8,128)} %bitcast.67), channel_id=1, source_target_pairs={{4,0},{8,4},{12,8},{16,12},{20,16},{24,20},{28,24},{0,28},{5,1},{9... | collective-permute-start | bytes 3686408 | tf_op jit(solution)/shard_map/ppermute | solution.py:30
  47.0 1.0 copy-start.7
  47.0 29.0 %collective-permute-start.2 = (f32[32,9600]{1,0:T(8,128)S(1)}, f32[32,9600]{1,0:T(8,128)}, u32[]{:S(2)}, u32[]{:S(2)}) collective-permute-start(f32[32,9600]{1,0:T(8,128)S(1)} %collective-permute-done.1), channel_id=1, source_target_pairs={{0,4},{4,8},{8,12},{12,16},{16,20},{20,24},{24,28},{28,0},{1,5},{5... | collective-permute-start | bytes 3686408 | tf_op jit(solution)/shard_map/ppermute | solution.py:28
  48.0 29.8 %collective-permute-start.5 = (f32[32,9600]{1,0:T(8,128)S(1)}, f32[32,9600]{1,0:T(8,128)}, u32[]{:S(2)}, u32[]{:S(2)}) collective-permute-start(f32[32,9600]{1,0:T(8,128)S(1)} %collective-permute-done.4), channel_id=1, source_target_pairs={{4,0},{8,4},{12,8},{16,12},{20,16},{24,20},{28,24},{0,28},{5,1},{9... | collective-permute-start | bytes 3686408 | tf_op jit(solution)/shard_map/ppermute | solution.py:30
  76.0 29.8 %collective-permute-start.3 = (f32[32,9600]{1,0:T(8,128)}, f32[32,9600]{1,0:T(8,128)}, u32[]{:S(2)}, u32[]{:S(2)}) collective-permute-start(f32[32,9600]{1,0:T(8,128)} %collective-permute-done.2), channel_id=1, source_target_pairs={{0,4},{4,8},{8,12},{12,16},{16,20},{20,24},{24,28},{28,0},{1,5},{5... | collective-permute-start | bytes 3686408 | tf_op jit(solution)/shard_map/ppermute | solution.py:28
  77.8 40.6 %collective-permute-start.6 = (f32[32,9600]{1,0:T(8,128)}, f32[32,9600]{1,0:T(8,128)S(1)}, u32[]{:S(2)}, u32[]{:S(2)}) collective-permute-start(f32[32,9600]{1,0:T(8,128)} %collective-permute-done.5), channel_id=1, source_target_pairs={{4,0},{8,4},{12,8},{16,12},{20,16},{24,20},{28,24},{0,28},{5,1},{9... | collective-permute-start | bytes 3686408 | tf_op jit(solution)/shard_map/ppermute | solution.py:30
  108.2 2.5 copy-start.8
  111.9 1.7 copy-start.6
  146.7 1.5 copy-start
  150.0 1.6 copy-start.1
  152.1 3.8 collective-permute-start.7
  152.5 4.0 collective-permute-start.8
  156.8 2.3 copy-start.2
  156.8 2.3 copy-start.3
  157.8 9.2 %collective-permute-start.10 = (f32[8,1,482]{2,1,0:T(1,128)S(1)}, f32[8,1,482]{2,1,0:T(1,128)S(1)}, u32[]{:S(2)}, u32[]{:S(2)}) collective-permute-start(f32[8,1,482]{2,1,0:T(1,128)S(1)} %get-tuple-element.16), channel_id=1, source_target_pairs={{1,0},{2,1},{3,2},{5,4},{6,5},{7,6},{9,8},{10,9},{11,10},{13,12},{... | collective-permute-start | bytes 46280 | tf_op jit(solution)/shard_map/ppermute | solution.py:45
  160.0 8.5 %collective-permute-start.9 = (f32[8,1,482]{2,1,0:T(1,128)S(1)}, f32[8,1,482]{2,1,0:T(1,128)S(1)}, u32[]{:S(2)}, u32[]{:S(2)}) collective-permute-start(f32[8,1,482]{2,1,0:T(1,128)S(1)} %get-tuple-element.15), channel_id=1, source_target_pairs={{0,1},{1,2},{2,3},{4,5},{5,6},{6,7},{8,9},{9,10},{10,11},{12,13},{... | collective-permute-start | bytes 46280 | tf_op jit(solution)/shard_map/ppermute | solution.py:44
  168.8 1.3 copy-start.5
  171.6 1.1 copy-start.4
  172.7 5.5 %collective-permute-start.11 = (f32[1,160,1]{2,1,0:T(8,128)S(1)}, f32[1,160,1]{2,1,0:T(8,128)S(1)}, u32[]{:S(2)}, u32[]{:S(2)}) collective-permute-start(f32[1,160,1]{2,1,0:T(8,128)S(1)} %get-tuple-element.31), channel_id=1, source_target_pairs={{0,4},{4,8},{8,12},{12,16},{16,20},{20,24},{24,28},{28,0},{1,5},{5... | collective-permute-start | bytes 1928 | tf_op jit(solution)/shard_map/ppermute | solution.py:44
  172.8 5.4 %collective-permute-start.12 = (f32[1,160,1]{2,1,0:T(8,128)S(1)}, f32[1,160,1]{2,1,0:T(8,128)S(1)}, u32[]{:S(2)}, u32[]{:S(2)}) collective-permute-start(f32[1,160,1]{2,1,0:T(8,128)S(1)} %get-tuple-element.32), channel_id=1, source_target_pairs={{4,0},{8,4},{12,8},{16,12},{20,16},{24,20},{28,24},{0,28},{5,1},{9... | collective-permute-start | bytes 1928 | tf_op jit(solution)/shard_map/ppermute | solution.py:45
  178.3 5.7 %collective-permute-start.13 = (f32[1,1,482]{2,1,0:T(1,128)S(1)}, f32[1,1,482]{2,1,0:T(1,128)S(1)}, u32[]{:S(2)}, u32[]{:S(2)}) collective-permute-start(f32[1,1,482]{2,1,0:T(1,128)S(1)} %get-tuple-element.25), channel_id=1, source_target_pairs={{0,1},{1,2},{2,3},{4,5},{5,6},{6,7},{8,9},{9,10},{10,11},{12,13},{... | collective-permute-start | bytes 5792 | tf_op jit(solution)/shard_map/ppermute | solution.py:44
  182.5 5.5 %collective-permute-start.14 = (f32[1,1,482]{2,1,0:T(1,128)S(1)}, f32[1,1,482]{2,1,0:T(1,128)S(1)}, u32[]{:S(2)}, u32[]{:S(2)}) collective-permute-start(f32[1,1,482]{2,1,0:T(1,128)S(1)} %get-tuple-element.26), channel_id=1, source_target_pairs={{1,0},{2,1},{3,2},{5,4},{6,5},{7,6},{9,8},{10,9},{11,10},{13,12},{... | collective-permute-start | bytes 5792 | tf_op jit(solution)/shard_map/ppermute | solution.py:45
  272.3 4.8 %collective-permute-start.15 = (f32[1,160,1]{2,1,0:T(8,128)S(1)}, f32[1,160,1]{2,1,0:T(8,128)S(1)}, u32[]{:S(2)}, u32[]{:S(2)}) collective-permute-start(f32[1,160,1]{2,1,0:T(8,128)S(1)} %get-tuple-element.29), channel_id=1, source_target_pairs={{0,4},{4,8},{8,12},{12,16},{16,20},{20,24},{24,28},{28,0},{1,5},{5... | collective-permute-start | bytes 1928 | tf_op jit(solution)/shard_map/ppermute | solution.py:44
  272.3 4.8 %collective-permute-start.16 = (f32[1,160,1]{2,1,0:T(8,128)S(1)}, f32[1,160,1]{2,1,0:T(8,128)S(1)}, u32[]{:S(2)}, u32[]{:S(2)}) collective-permute-start(f32[1,160,1]{2,1,0:T(8,128)S(1)} %get-tuple-element.30), channel_id=1, source_target_pairs={{4,0},{8,4},{12,8},{16,12},{20,16},{24,20},{28,24},{0,28},{5,1},{9... | collective-permute-start | bytes 1928 | tf_op jit(solution)/shard_map/ppermute | solution.py:45
  277.2 4.9 %collective-permute-start.17 = (f32[1,1,482]{2,1,0:T(1,128)S(1)}, f32[1,1,482]{2,1,0:T(1,128)S(1)}, u32[]{:S(2)}, u32[]{:S(2)}) collective-permute-start(f32[1,1,482]{2,1,0:T(1,128)S(1)} %get-tuple-element.23), channel_id=1, source_target_pairs={{0,1},{1,2},{2,3},{4,5},{5,6},{6,7},{8,9},{9,10},{10,11},{12,13},{... | collective-permute-start | bytes 5792 | tf_op jit(solution)/shard_map/ppermute | solution.py:44
  280.8 5.5 %collective-permute-start.18 = (f32[1,1,482]{2,1,0:T(1,128)S(1)}, f32[1,1,482]{2,1,0:T(1,128)S(1)}, u32[]{:S(2)}, u32[]{:S(2)}) collective-permute-start(f32[1,1,482]{2,1,0:T(1,128)S(1)} %get-tuple-element.24), channel_id=1, source_target_pairs={{1,0},{2,1},{3,2},{5,4},{6,5},{7,6},{9,8},{10,9},{11,10},{13,12},{... | collective-permute-start | bytes 5792 | tf_op jit(solution)/shard_map/ppermute | solution.py:45
  372.1 4.8 %collective-permute-start.19 = (f32[1,160,1]{2,1,0:T(8,128)S(1)}, f32[1,160,1]{2,1,0:T(8,128)S(1)}, u32[]{:S(2)}, u32[]{:S(2)}) collective-permute-start(f32[1,160,1]{2,1,0:T(8,128)S(1)} %get-tuple-element.27), channel_id=1, source_target_pairs={{0,4},{4,8},{8,12},{12,16},{16,20},{20,24},{24,28},{28,0},{1,5},{5... | collective-permute-start | bytes 1928 | tf_op jit(solution)/shard_map/ppermute | solution.py:44
  372.2 4.8 %collective-permute-start.20 = (f32[1,160,1]{2,1,0:T(8,128)S(1)}, f32[1,160,1]{2,1,0:T(8,128)S(1)}, u32[]{:S(2)}, u32[]{:S(2)}) collective-permute-start(f32[1,160,1]{2,1,0:T(8,128)S(1)} %get-tuple-element.28), channel_id=1, source_target_pairs={{4,0},{8,4},{12,8},{16,12},{20,16},{24,20},{28,24},{0,28},{5,1},{9... | collective-permute-start | bytes 1928 | tf_op jit(solution)/shard_map/ppermute | solution.py:45
  377.0 4.6 %collective-permute-start.21 = (f32[1,1,482]{2,1,0:T(1,128)S(1)}, f32[1,1,482]{2,1,0:T(1,128)S(1)}, u32[]{:S(2)}, u32[]{:S(2)}) collective-permute-start(f32[1,1,482]{2,1,0:T(1,128)S(1)} %get-tuple-element.21), channel_id=1, source_target_pairs={{0,1},{1,2},{2,3},{4,5},{5,6},{6,7},{8,9},{9,10},{10,11},{12,13},{... | collective-permute-start | bytes 5792 | tf_op jit(solution)/shard_map/ppermute | solution.py:44
  380.3 5.5 %collective-permute-start.22 = (f32[1,1,482]{2,1,0:T(1,128)S(1)}, f32[1,1,482]{2,1,0:T(1,128)S(1)}, u32[]{:S(2)}, u32[]{:S(2)}) collective-permute-start(f32[1,1,482]{2,1,0:T(1,128)S(1)} %get-tuple-element.22), channel_id=1, source_target_pairs={{1,0},{2,1},{3,2},{5,4},{6,5},{7,6},{9,8},{10,9},{11,10},{13,12},{... | collective-permute-start | bytes 5792 | tf_op jit(solution)/shard_map/ppermute | solution.py:45
